TPU v7x, 32 devices: a whole 2x2x4 slice. The times are simulated.
32 devices in a mesh: sec: 4 (over y, x), seq: 8 (over z, core).
Axes of the slice: x: 2, y: 2, z: 4, core: 2. Of those that a mesh axis runs over, the one named last changes fastest.
Arguments:
- long_queries: bfloat16 [16, 4096], P('sec'), may hold values from -15 to 15
- long_keys: bfloat16 [512, 16, 2048], P(('sec', 'seq')), may hold values from -6 to 6
- long_values: bfloat16 [512, 16, 2048], P(('sec', 'seq')), may hold values from -6 to 6
- page_table: int32 [16, 32], replicated, may hold values from 0 to 511, as said below
- long_lengths: int32 [16], replicated, may hold values from 1 to 512, 5120 in all
- short_queries: bfloat16 [32, 256], P(('sec', 'seq')), may hold values from -15 to 15
- short_keys: bfloat16 [32, 2048, 128], P(('sec', 'seq')), may hold values from -6 to 6
- short_values: bfloat16 [32, 2048, 128], P(('sec', 'seq')), may hold values from -6 to 6
- short_lengths: int32 [2], replicated, may hold values from 1 to 2048, 2560 in all
- out_weight: bfloat16 [4096, 4608], P('seq', 'sec'), may hold values from -0.09375 to 0.09375
- long_resid: bfloat16 [16, 4608], P(None, 'sec'), may hold values from -1.5 to 1.5
Outputs:
- long_out: bfloat16 [16, 4608], P(None, 'sec')
- short_out: bfloat16 [32, 256], P(('sec', 'seq'))
Inputs may be any that keep to these rules, and one draw needn't show every extreme that they name: `page_table`: row r lists the 32 pool pages of long request r in order of position; every page of the pool of 512 appears exactly once; page g is held by device g // 16 along sec+seq. `long_lengths`: counts the newest token; later slots are unused. `short_lengths`: counts the newest token; later slots are unused.
All inputs are finite; a program needn't handle non-finite values.
Results may differ from a plain program's by a relative error of at most 0.0055.
Values may be sent and summed in bfloat16 or wider, within the bound.
A program may use at most 64 MiB of HBM per device.

v0:
```python
import jax
import jax.numpy as jnp
from jax import lax
from jax.sharding import PartitionSpec as P

KVH = 16
HD = 128
G = 2
soft_cap = 50.0
score_scale = 144.0 ** (-0.5)


def capped_weights(raw_scores, live_mask):
    capped = soft_cap * jnp.tanh(raw_scores * (score_scale / soft_cap))
    return jnp.where(live_mask, jnp.exp(capped), 0.0)


def per_device(
    long_queries,
    long_keys,
    long_values,
    page_table,
    long_lengths,
    short_queries,
    short_keys,
    short_values,
    short_lengths,
    out_weight,
    long_resid,
):
    queries = lax.all_gather(long_queries, "sec", axis=0, tiled=True)
    requests = queries.shape[0]
    page_count, page_len, kv_width = long_keys.shape
    tokens = page_count * page_len
    head_count = KVH * G
    first_page = lax.axis_index(("sec", "seq")) * page_count
    page_ids = first_page + jnp.arange(page_count, dtype=jnp.int32)
    matched = page_table[:, :, None] == page_ids[None, None, :]
    page_held = jnp.any(matched, axis=1)
    slot_index = jnp.arange(page_table.shape[1], dtype=jnp.int32)
    slot_of = jnp.sum(jnp.where(matched, slot_index[None, :, None], 0), axis=1)
    position = slot_of[:, :, None] * page_len + jnp.arange(page_len, dtype=jnp.int32)[None, None, :]
    live_mask = page_held[:, :, None] & (position < long_lengths[:, None, None])
    live_mask = live_mask.reshape(requests, tokens)
    grouped = (
        queries.reshape(requests, KVH, G, HD).transpose(1, 0, 2, 3).reshape(KVH, requests * G, HD)
    )
    key_rows = long_keys.reshape(tokens, KVH, HD)
    value_rows = long_values.reshape(tokens, KVH, HD)
    raw_scores = jnp.einsum("hqd,thd->hqt", grouped, key_rows, preferred_element_type=jnp.float32)
    token_mask = jnp.broadcast_to(live_mask[None, :, None, :], (KVH, requests, G, tokens)).reshape(
        KVH, requests * G, tokens
    )
    weights = capped_weights(raw_scores, token_mask)
    totals = jnp.sum(weights, axis=2)
    part_sums = jnp.einsum(
        "hqt,thd->hqd", weights.astype(jnp.bfloat16), value_rows, preferred_element_type=jnp.float32
    )
    part_sums = (
        part_sums.reshape(KVH, requests, G, HD)
        .transpose(1, 0, 2, 3)
        .reshape(requests, head_count * HD)
    )
    totals = totals.reshape(KVH, requests, G).transpose(1, 0, 2).reshape(requests, head_count)
    share_width = out_weight.shape[0]
    share_start = lax.axis_index("seq") * share_width
    part_sums, totals = lax.psum((part_sums, totals), ("sec", "seq"))
    attention = (
        (part_sums.reshape(requests, head_count, HD) / totals[:, :, None])
        .astype(jnp.bfloat16)
        .reshape(requests, head_count * HD)
    )
    feature_rows = lax.dynamic_slice_in_dim(attention, share_start, share_width, 1)
    partial_proj = jnp.dot(feature_rows, out_weight, preferred_element_type=jnp.float32)
    projected = lax.psum(partial_proj, "seq")
    long_out = (long_resid.astype(jnp.float32) + projected).astype(jnp.bfloat16)
    pair_count = short_queries.shape[0]
    length = short_keys.shape[1]
    pair_ids = lax.axis_index(("sec", "seq")) * pair_count + jnp.arange(pair_count, dtype=jnp.int32)
    request_of = pair_ids // KVH
    chosen = request_of[:, None] == jnp.arange(short_lengths.shape[0], dtype=jnp.int32)[None, :]
    pair_limit = jnp.sum(jnp.where(chosen, short_lengths[None, :], 0), axis=1)
    short_live = jnp.arange(length, dtype=jnp.int32)[None, :] < pair_limit[:, None]
    pair_queries = short_queries.reshape(pair_count, G, HD)
    short_scores = jnp.einsum(
        "pgd,ptd->pgt", pair_queries, short_keys, preferred_element_type=jnp.float32
    )
    short_weights = capped_weights(short_scores, short_live[:, None, :])
    short_totals = jnp.sum(short_weights, axis=2)
    short_sums = jnp.einsum(
        "pgt,ptd->pgd",
        short_weights.astype(jnp.bfloat16),
        short_values,
        preferred_element_type=jnp.float32,
    )
    short_out = (
        (short_sums / short_totals[:, :, None]).astype(jnp.bfloat16).reshape(pair_count, G * HD)
    )
    return (long_out, short_out)


def solution(mesh):
    in_specs = (
        P("sec", None),
        P(("sec", "seq"), None, None),
        P(("sec", "seq"), None, None),
        P(),
        P(),
        P(("sec", "seq"), None),
        P(("sec", "seq"), None, None),
        P(("sec", "seq"), None, None),
        P(),
        P("seq", "sec"),
        P(None, "sec"),
    )
    out_specs = (P(None, "sec"), P(("sec", "seq"), None))
    return jax.shard_map(
        per_device, mesh=mesh, in_specs=in_specs, out_specs=out_specs, check_vma=False
    )
```

profile of v0, /device:TPU:8, one launch (start us, length us, event | category | flops | bytes accessed | tf_op | source)
XLA Modules:
  0.0 212.9 jit_solution(14925022806387552283)
XLA Ops:
  7.2 0.0 copy-start
  7.2 0.0 all-reduce.3.cloned.1.call-start
  7.2 1.2 fusion.16
  8.4 1.1 compare_reduce_fusion
  9.6 0.1 add.56
  9.7 0.0 copy-start.4
  9.7 0.1 add.57
  9.8 0.1 and.21
  9.9 0.1 and.22
  10.0 0.1 add.59
  10.1 0.7 fusion.20
  10.9 0.0 copy-start.1
  10.9 1.5 copy.36
  12.5 0.0 copy-done.4
  12.5 8.5 %all-gather = bf16[4,4,4096]{2,1,0:T(4,128)(2,1)S(1)} all-gather(bf16[1,4,4096]{2,1,0:T(4,128)(2,1)S(1)} %bitcast.58), channel_id=1, replica_groups=mesh['sec'=4,'seq'=8] {'sec'}, dimensions={0}, use_global_device_ids=true | all-gather | bytes 163840 | tf_op jit(solution)/shard_map/all_gather | solution.py:31
  20.9 0.2 reshape.129
  21.1 0.1 copy.29
  21.2 0.0 copy-done.1
  21.2 0.2 copy.37
  21.4 0.6 fusion.25
  22.0 0.0 copy-start.7
  22.0 0.3 fusion.10
  22.4 0.0 copy-start.5
  22.4 0.0 copy-start.2
  22.4 0.1 copy.50
  22.5 0.9 reshape.134
  23.4 0.0 all-reduce.3.cloned.1.call-update
  23.5 0.0 all-reduce.5.cloned.1.call-start
  23.5 0.0 copy-done.7
  23.5 0.6 fusion.22
  24.2 0.7 iota_compare_fusion
  24.8 0.1 copy.33
  24.9 0.1 copy.34
  25.0 39.6 %psum.22 = f32[16,32]{0,1:T(8,128)S(1)} all-reduce(f32[16,32]{0,1:T(8,128)S(1)} %bitcast.57), channel_id=1, replica_groups=mesh['sec'=4,'seq'=8] {'sec','seq'}, use_global_device_ids=true, to_apply=%region_4.5 | all-reduce | flops 512 | bytes 4096 | tf_op jit(solution)/shard_map/psum | solution.py:67
  64.6 0.1 copy.35
  64.7 0.1 div.30
  64.8 0.0 copy-start.6
  64.8 0.2 copy.49
  65.0 0.0 copy-done.5
  65.0 0.0 copy-done.2
  65.0 0.0 copy-start.3
  65.0 0.4 fusion.26
  65.4 85.0 %all-reduce.3.cloned.1.call-done = f32[16,4096]{1,0:T(8,128)} async-done(((f32[16,4096]{1,0:T(8,128)}), f32[16,4096]{1,0:T(8,128)}) %all-reduce.3.cloned.1.call-update) | async-done | bytes 262160 | tf_op jit(solution)/shard_map/psum | solution.py:67
  150.4 0.0 copy-done
  150.4 1.6 fusion.18
  152.1 0.0 all-reduce.5.cloned.1.call-update
  152.1 0.0 copy-done.6
  152.1 0.2 fusion.9
  152.3 0.6 copy.51
  152.9 51.7 %all-reduce.5.cloned.1.call-done = f32[16,1152]{1,0:T(8,128)} async-done(((f32[16,1152]{1,0:T(8,128)}), f32[16,1152]{1,0:T(8,128)}) %all-reduce.5.cloned.1.call-update) | async-done | bytes 73744 | tf_op jit(solution)/shard_map/psum | solution.py:75
  204.5 0.0 copy-done.3
  204.5 1.5 add_convert_fusion
  (6 shorter events, 0.1 us)
Async XLA Ops:
  7.2 143.3 %copy-start = (bf16[512,1152]{1,0:T(8,128)(2,1)S(1)}, bf16[512,1152]{1,0:T(8,128)(2,1)}, u32[]{:S(2)}) copy-start(bf16[512,1152]{1,0:T(8,128)(2,1)} %param.20) | copy-start | bytes 3538948
  7.2 143.2 %all-reduce.3.cloned.1.call-start = ((), (), s32[]{:S(2)}) async-start(), calls=%async_computation | async-start | bytes 524288 | tf_op jit(solution)/shard_map/psum | solution.py:67
  9.7 2.8 %copy-start.4 = (bf16[4,4096]{1,0:T(4,128)(2,1)S(1)}, bf16[4,4096]{1,0:T(4,128)(2,1)}, u32[]{:S(2)}) copy-start(bf16[4,4096]{1,0:T(4,128)(2,1)} %param.11) | copy-start | bytes 98308
  10.9 10.3 %copy-start.1 = (bf16[16,16,2048]{2,1,0:T(8,128)(2,1)S(1)}, bf16[16,16,2048]{2,1,0:T(8,128)(2,1)}, u32[]{:S(2)}) copy-start(bf16[16,16,2048]{2,1,0:T(8,128)(2,1)} %param.13) | copy-start | bytes 3145732
  22.0 1.5 copy-start.7
  22.4 42.6 %copy-start.5 = (bf16[1,256]{1,0:T(2,128)(2,1)S(1)}, bf16[1,256]{1,0:T(2,128)(2,1)}, u32[]{:S(2)}) copy-start(bf16[1,256]{1,0:T(2,128)(2,1)} %param.16) | copy-start | bytes 1540
  22.4 42.6 %copy-start.2 = (bf16[1,2048,128]{2,1,0:T(8,128)(2,1)S(1)}, bf16[1,2048,128]{2,1,0:T(8,128)(2,1)}, u32[]{:S(2)}) copy-start(bf16[1,2048,128]{2,1,0:T(8,128)(2,1)} %param.17) | copy-start | bytes 1572868
  23.5 181.1 %all-reduce.5.cloned.1.call-start = ((), (), s32[]{:S(2)}) async-start(), calls=%async_computation.1 | async-start | bytes 147456 | tf_op jit(solution)/shard_map/psum | solution.py:75
  64.8 87.3 %copy-start.6 = (bf16[1,2048,128]{2,1,0:T(8,128)(2,1)S(1)}, bf16[1,2048,128]{2,1,0:T(8,128)(2,1)}, u32[]{:S(2)}) copy-start(bf16[1,2048,128]{2,1,0:T(8,128)(2,1)} %param.18) | copy-start | bytes 1572868
  65.0 139.5 %copy-start.3 = (bf16[16,1152]{1,0:T(8,128)(2,1)S(1)}, bf16[16,1152]{1,0:T(8,128)(2,1)}, u32[]{:S(2)}) copy-start(bf16[16,1152]{1,0:T(8,128)(2,1)} %param.21) | copy-start | bytes 110596
Sparse Core Ops, SparseCore 0:
  23.6 126.7 all-reduce.2
  152.8 51.7 all-reduce.4
where the time goes:
time: 213 us
  waiting for transfers between devices  137 us (64%)
  blocking collectives  48.1 us (23%)
  between operations  14.3 us (7%)
  other arithmetic  5.86 us (3%)
  local copies, waits for them, and re-layouts  4.75 us (2%)
  matrix products  3.13 us (1%)
    psum x1, waiting for transfers between devices, per_device(): part_sums, totals = lax.psum((part_sums, totals), ('sec', 'seq'))  85 us
    psum x1, waiting for transfers between devices, per_device(): projected = lax.psum(partial_proj, 'seq')  51.7 us
    psum x1, blocking collectives, per_device(): part_sums, totals = lax.psum((part_sums, totals), ('sec', 'seq'))  39.6 us
    all_gather x1, blocking collectives, per_device(): queries = lax.all_gather(long_queries, 'sec', axis=0, tiled=True)  8.46 us
  transfers between devices with their start and end apart: 2, of which 2 were waited for; matrix products, arithmetic and copies ran while one was open for 1% of the time, Pallas kernels for 0%

commit v1 on v0

--- a/solution.py
+++ b/solution.py
@@ -8,6 +8,15 @@
 G = 2
 soft_cap = 50.0
 score_scale = 144.0 ** (-0.5)
+
+
+def doubling_sum(value, axis):
+    peers = lax.axis_size(axis)
+    summed, far = (value, 1)
+    while far < peers:
+        summed = summed + lax.ppermute(summed, axis, [(i, i ^ far) for i in range(peers)])
+        far = 2 * far
+    return summed
 
 
 def capped_weights(raw_scores, live_mask):
@@ -72,7 +81,7 @@
     )
     feature_rows = lax.dynamic_slice_in_dim(attention, share_start, share_width, 1)
     partial_proj = jnp.dot(feature_rows, out_weight, preferred_element_type=jnp.float32)
-    projected = lax.psum(partial_proj, "seq")
+    projected = doubling_sum(partial_proj, "seq")
     long_out = (long_resid.astype(jnp.float32) + projected).astype(jnp.bfloat16)
     pair_count = short_queries.shape[0]
     length = short_keys.shape[1]

time: 213 us -> 172 us (0.81)
  waiting for transfers between devices: 137 us -> 93.4 us
    psum x1 -> x0, waiting for transfers between devices: 51.7 us -> none  [per_device(): projected = lax.psum(partial_proj, 'seq')]
    ppermute x0 -> x3, waiting for transfers between devices: none -> 7.07 us  [doubling_sum(): lax.ppermute(summed, axis, [(i, i ^ far) for i in range(peers)])]
    ppermute x0 -> x3, starting transfers between devices: none -> 2.14 us  [doubling_sum(): lax.ppermute(summed, axis, [(i, i ^ far) for i in range(peers)])]
  transfers between devices with their start and end apart: 2 -> 4, of which waited for: 2 -> 4; matrix products, arithmetic and copies ran while one was open for 1% -> 2% of each run, Pallas kernels for 0% -> 0%
where the time goes in v1:
time: 172 us; the launch traced here: 170 us
  waiting for transfers between devices  93.4 us (54%)
  blocking collectives  47.9 us (28%)
  between operations  14.3 us (8%)
  other arithmetic  5.01 us (3%)
  local copies, waits for them, and re-layouts  4.75 us (3%)
  matrix products  2.5 us (1%)
  starting transfers between devices  2.18 us (1%)
    psum x1, waiting for transfers between devices, per_device(): part_sums, totals = lax.psum((part_sums, totals), ('sec', 'seq'))  86.3 us
    psum x1, blocking collectives, per_device(): part_sums, totals = lax.psum((part_sums, totals), ('sec', 'seq'))  39.5 us
    all_gather x1, blocking collectives, per_device(): queries = lax.all_gather(long_queries, 'sec', axis=0, tiled=True)  8.46 us
    ppermute x3, waiting for transfers between devices, doubling_sum(): lax.ppermute(summed, axis, [(i, i ^ far) for i in range(peers)])  7.07 us
  transfers between devices with their start and end apart: 4, of which 4 were waited for; matrix products, arithmetic and copies ran while one was open for 2% of the time, Pallas kernels for 0%

profile of v1, /device:TPU:8, one launch (start us, length us, event | category | flops | bytes accessed | tf_op | source)
XLA Modules:
  0.0 170.0 jit_solution(15663106101753935062)
XLA Ops:
  7.2 0.0 copy-start
  7.2 0.0 all-reduce.2.cloned.1.call-start
  7.2 1.2 fusion.16
  8.4 1.1 compare_reduce_fusion
  9.6 0.1 add.63
  9.7 0.0 copy-start.4
  9.7 0.1 add.64
  9.8 0.1 and.21
  9.9 0.1 and.22
  10.0 0.1 add.66
  10.1 0.7 fusion.20
  10.9 0.0 copy-start.1
  10.9 1.5 copy.36
  12.5 0.0 copy-done.4
  12.5 8.5 %all-gather = bf16[4,4,4096]{2,1,0:T(4,128)(2,1)S(1)} all-gather(bf16[1,4,4096]{2,1,0:T(4,128)(2,1)S(1)} %bitcast.58), channel_id=1, replica_groups=mesh['sec'=4,'seq'=8] {'sec'}, dimensions={0}, use_global_device_ids=true | all-gather | bytes 163840 | tf_op jit(solution)/shard_map/all_gather | solution.py:40
  20.9 0.2 reshape.129
  21.1 0.1 copy.29
  21.2 0.0 copy-done.1
  21.2 0.2 copy.37
  21.4 0.6 fusion.25
  22.0 0.3 fusion.10
  22.4 0.0 copy-start.5
  22.4 0.0 copy-start.7
  22.4 0.1 copy.50
  22.5 0.9 reshape.134
  23.4 0.0 all-reduce.2.cloned.1.call-update
  23.5 0.1 copy.33
  23.5 0.1 copy.34
  23.6 39.5 %psum.15 = f32[16,32]{0,1:T(8,128)S(1)} all-reduce(f32[16,32]{0,1:T(8,128)S(1)} %bitcast.57), channel_id=1, replica_groups=mesh['sec'=4,'seq'=8] {'sec','seq'}, use_global_device_ids=true, to_apply=%region_4.5 | all-reduce | flops 512 | bytes 4096 | tf_op jit(solution)/shard_map/psum | solution.py:76
  63.1 0.1 copy.35
  63.2 0.0 copy-start.2
  63.2 0.1 div.30
  63.3 0.2 copy.49
  63.5 0.0 copy-start.6
  63.5 0.0 copy-done.5
  63.5 0.0 copy-done.7
  63.6 0.6 fusion.22
  64.2 86.3 %all-reduce.2.cloned.1.call-done = f32[16,4096]{1,0:T(8,128)} async-done(((f32[16,4096]{1,0:T(8,128)}), f32[16,4096]{1,0:T(8,128)}) %all-reduce.2.cloned.1.call-update) | async-done | bytes 262160 | tf_op jit(solution)/shard_map/psum | solution.py:76
  150.5 0.0 copy-done
  150.5 0.0 copy-start.3
  150.5 1.0 fusion.18
  151.5 0.0 collective-permute-start
  151.5 0.7 iota_compare_fusion
  152.2 0.6 collective-permute-done
  152.8 0.6 collective-permute-start.1
  153.4 0.0 copy-done.2
  153.4 0.4 fusion.26
  153.8 3.4 %collective-permute-done.1 = f32[16,1152]{1,0:T(8,128)S(1)} collective-permute-done((f32[16,1152]{1,0:T(8,128)S(1)}, f32[16,1152]{1,0:T(8,128)S(1)}, u32[]{:S(2)}, u32[]{:S(2)}) %collective-permute-start.1) | collective-permute-done | bytes 73760 | tf_op jit(solution)/shard_map/ppermute | solution.py:17
  157.2 1.5 collective-permute-start.2
  158.7 0.0 copy-done.6
  158.7 0.2 fusion.9
  158.9 0.6 copy.51
  159.5 3.0 %collective-permute-done.2 = f32[16,1152]{1,0:T(8,128)S(1)} collective-permute-done((f32[16,1152]{1,0:T(8,128)S(1)}, f32[16,1152]{1,0:T(8,128)S(1)}, u32[]{:S(2)}, u32[]{:S(2)}) %collective-permute-start.2) | collective-permute-done | bytes 73760 | tf_op jit(solution)/shard_map/ppermute | solution.py:17
  162.5 0.0 copy-done.3
  162.5 0.6 add_convert_fusion
  (8 shorter events, 0.1 us)
Async XLA Ops:
  7.2 143.3 %copy-start = (bf16[512,1152]{1,0:T(8,128)(2,1)S(1)}, bf16[512,1152]{1,0:T(8,128)(2,1)}, u32[]{:S(2)}) copy-start(bf16[512,1152]{1,0:T(8,128)(2,1)} %param.20) | copy-start | bytes 3538948
  7.2 143.3 %all-reduce.2.cloned.1.call-start = ((), (), s32[]{:S(2)}) async-start(), calls=%async_computation | async-start | bytes 524288 | tf_op jit(solution)/shard_map/psum | solution.py:76
  9.7 2.8 %copy-start.4 = (bf16[4,4096]{1,0:T(4,128)(2,1)S(1)}, bf16[4,4096]{1,0:T(4,128)(2,1)}, u32[]{:S(2)}) copy-start(bf16[4,4096]{1,0:T(4,128)(2,1)} %param.11) | copy-start | bytes 98308
  10.9 10.3 %copy-start.1 = (bf16[16,16,2048]{2,1,0:T(8,128)(2,1)S(1)}, bf16[16,16,2048]{2,1,0:T(8,128)(2,1)}, u32[]{:S(2)}) copy-start(bf16[16,16,2048]{2,1,0:T(8,128)(2,1)} %param.13) | copy-start | bytes 3145732
  22.4 41.1 %copy-start.5 = (bf16[1,256]{1,0:T(2,128)(2,1)S(1)}, bf16[1,256]{1,0:T(2,128)(2,1)}, u32[]{:S(2)}) copy-start(bf16[1,256]{1,0:T(2,128)(2,1)} %param.16) | copy-start | bytes 1540
  22.4 41.2 %copy-start.7 = (s32[2]{0:T(128)S(1)}, s32[2]{0:T(128)}, u32[]{:S(2)}) copy-start(s32[2]{0:T(128)} %param.19) | copy-start | bytes 28
  63.2 90.2 %copy-start.2 = (bf16[1,2048,128]{2,1,0:T(8,128)(2,1)S(1)}, bf16[1,2048,128]{2,1,0:T(8,128)(2,1)}, u32[]{:S(2)}) copy-start(bf16[1,2048,128]{2,1,0:T(8,128)(2,1)} %param.17) | copy-start | bytes 1572868
  63.5 95.2 %copy-start.6 = (bf16[1,2048,128]{2,1,0:T(8,128)(2,1)S(1)}, bf16[1,2048,128]{2,1,0:T(8,128)(2,1)}, u32[]{:S(2)}) copy-start(bf16[1,2048,128]{2,1,0:T(8,128)(2,1)} %param.18) | copy-start | bytes 1572868
  150.5 12.1 %copy-start.3 = (bf16[16,1152]{1,0:T(8,128)(2,1)S(1)}, bf16[16,1152]{1,0:T(8,128)(2,1)}, u32[]{:S(2)}) copy-start(bf16[16,1152]{1,0:T(8,128)(2,1)} %param.21) | copy-start | bytes 110596
  151.5 1.3 collective-permute-start
  152.8 4.4 %collective-permute-start.1 = (f32[16,1152]{1,0:T(8,128)S(1)}, f32[16,1152]{1,0:T(8,128)S(1)}, u32[]{:S(2)}, u32[]{:S(2)}) collective-permute-start(f32[16,1152]{1,0:T(8,128)S(1)} %add.70), channel_id=1, source_target_pairs={{0,2},{1,3},{2,0},{3,1},{4,6},{5,7},{6,4},{7,5},{8,10},{9,11},{10,... | collective-permute-start | bytes 221192 | tf_op jit(solution)/shard_map/ppermute | solution.py:17
  157.2 5.3 %collective-permute-start.2 = (f32[16,1152]{1,0:T(8,128)S(1)}, f32[16,1152]{1,0:T(8,128)S(1)}, u32[]{:S(2)}, u32[]{:S(2)}) collective-permute-start(f32[16,1152]{1,0:T(8,128)S(1)} %add.71), channel_id=1, source_target_pairs={{0,4},{1,5},{2,6},{3,7},{4,0},{5,1},{6,2},{7,3},{8,12},{9,13},{10,... | collective-permute-start | bytes 221192 | tf_op jit(solution)/shard_map/ppermute | solution.py:17
Sparse Core Ops, SparseCore 0:
  23.6 126.8 all-reduce.1
